TPU v7x, 32 devices: a whole 2x2x4 slice. The times are simulated.
32 devices in a mesh: ia: 8 (over z, y), ja: 4 (over x, core).
Axes of the slice: x: 2, y: 2, z: 4, core: 2. Of those that a mesh axis runs over, the one named last changes fastest.
Arguments:
- basis: bfloat16 [16, 8, 1024, 256], P('ia', 'ja'), may hold values from -0.1875 to 0.1875
- amplitudes: float32 [16, 8, 256, 256], P('ia', 'ja'), may hold values from -6 to 6
- integrals: float32 [16, 8, 256, 256], P('ia', 'ja'), may hold values from -6 to 6
- virt_energy: float32 [1024], replicated, may hold values from 0.05 to 2
- fock: float32 [16, 16], replicated, may hold values from -3 to 3
- occ_energy: float32 [8], P('ja'), may hold values from -2 to -0.2
- blocks: int32 [16, 8], P(None, 'ja'), may hold values from 1 to 2
- couplings: int32 [16, 8, 4], P(None, 'ja'), may hold values from 0 to 15, as said below
Outputs:
- new_amplitudes: float32 [16, 8, 256, 256], P('ia', 'ja')
Inputs may be any that keep to these rules, and one draw needn't show every extreme that they name: `couplings`: A pair's 4 entries name different k, none equal to the pair's own i, and no two in the same block of 2 consecutive first orbitals held by one index of ia. Of the 16 entries of the pairs that one device holds, exactly 2 name a k in each such block.
All inputs are finite; a program needn't handle non-finite values.
Results may differ from a plain program's by a relative error of at most 0.0031.
Values may be sent and summed in bfloat16 or wider, within the bound.
A program may use at most 128 MiB of HBM per device.

v0:
```python
import jax
import jax.numpy as jnp
from jax import lax
from jax.sharding import PartitionSpec as P

BLOCK = 128
NCOUPLE = 4
SWEEPS = 2


clip_share = 0.4
denominator_floor = 1.0


def rank_within(block_ids):
    entries = block_ids.shape[-1]
    matching = block_ids[..., :, None] == block_ids[..., None, :]
    earlier = jnp.arange(entries)[:, None] > jnp.arange(entries)[None, :]
    return jnp.sum((matching & earlier).astype(jnp.int32), axis=-1)


def shards(basis, amplitudes, integrals, virt_energy, fock, occ_energy, blocks, couplings):
    rows_here = basis.shape[0]
    columns_here = basis.shape[1]
    projected = basis.shape[2]
    pair_width = basis.shape[3]
    pairs_here = rows_here * columns_here
    requests = NCOUPLE * pairs_here
    row_groups = lax.axis_size("ia")
    column_groups = lax.axis_size("ja")
    slot_count = requests // row_groups
    group_index = lax.axis_index("ia")
    first_row = group_index * rows_here
    total_pairs = rows_here * row_groups * columns_here * column_groups
    local_blocks = lax.dynamic_slice_in_dim(blocks, first_row, rows_here, 0)
    orbital_index = jnp.arange(pair_width, dtype=jnp.int32)
    column_mask = orbital_index[None, None, :] < (local_blocks * BLOCK)[:, :, None]
    masked_grid = basis * column_mask[:, :, None, :].astype(jnp.bfloat16)
    masked = masked_grid.reshape(pairs_here, projected, pair_width)
    pair_mask = (
        (column_mask[:, :, :, None] & column_mask[:, :, None, :])
        .astype(jnp.float32)
        .reshape(pairs_here, pair_width, pair_width)
    )
    local_couplings = lax.dynamic_slice_in_dim(couplings, first_row, rows_here, 0)
    local_targets = local_couplings.reshape(requests) // rows_here
    arrival = local_targets * slot_count + rank_within(local_targets)
    all_couplings = couplings.reshape(row_groups, requests)
    all_targets = all_couplings // rows_here
    all_ranks = rank_within(all_targets)
    pair_column = jnp.arange(requests, dtype=jnp.int32) // NCOUPLE % columns_here
    source_pair = (all_couplings - first_row) * columns_here + pair_column[None, :]
    slot_index = jnp.arange(slot_count, dtype=jnp.int32)
    chosen = (all_targets == group_index)[:, :, None] & (
        all_ranks[:, :, None] == slot_index[None, None, :]
    )
    sources = jnp.sum(chosen.astype(jnp.int32) * source_pair[:, :, None], axis=1).reshape(
        row_groups * slot_count
    )
    fock_rows = lax.dynamic_slice_in_dim(fock, first_row, rows_here, 0)
    selector = (
        local_couplings[:, :, :, None]
        == jnp.arange(fock.shape[1], dtype=jnp.int32)[None, None, None, :]
    ).astype(jnp.float32)
    weights = jnp.sum(selector * fock_rows[:, None, None, :], axis=-1).reshape(pairs_here, NCOUPLE)
    occupied_diag = lax.dynamic_slice_in_dim(jnp.diagonal(fock), first_row, rows_here, 0)
    energy_shift = (occupied_diag[:, None] + occ_energy[None, :]).reshape(pairs_here)
    scaled = (masked.astype(jnp.float32) * virt_energy[None, :, None]).astype(jnp.bfloat16)
    virtual = jnp.einsum("pxa,pxb->pab", masked, scaled, preferred_element_type=jnp.float32)
    diagonal_part = jnp.diagonal(virtual, axis1=1, axis2=2)
    virtual_block = virtual.astype(jnp.bfloat16)
    denominators = jnp.maximum(
        diagonal_part[:, :, None] + diagonal_part[:, None, :] - energy_shift[:, None, None],
        denominator_floor,
    )
    current = amplitudes.reshape(pairs_here, pair_width, pair_width) * pair_mask
    pair_integrals = integrals.reshape(pairs_here, pair_width, pair_width)
    sent_bases = jnp.take(masked, sources, axis=0)
    arrived_bases = lax.all_to_all(sent_bases, "ia", split_axis=0, concat_axis=0, tiled=True)
    partners = jnp.take(arrived_bases, arrival, axis=0).reshape(
        pairs_here, NCOUPLE, projected, pair_width
    )
    intersection = jnp.einsum(
        "pxa,psxb->psab", masked, partners, preferred_element_type=jnp.float32
    ).astype(jnp.bfloat16)
    for sweep_index in range(SWEEPS):
        rounded = current.astype(jnp.bfloat16)
        sent_amplitudes = jnp.take(rounded, sources, axis=0)
        arrived_amplitudes = lax.all_to_all(
            sent_amplitudes, "ia", split_axis=0, concat_axis=0, tiled=True
        )
        local_terms = jnp.einsum(
            "pab,pbc->pac", virtual_block, rounded, preferred_element_type=jnp.float32
        )
        local_terms = local_terms + jnp.einsum(
            "pab,pbc->pac", rounded, virtual_block, preferred_element_type=jnp.float32
        )
        partner_amplitudes = jnp.take(arrived_amplitudes, arrival, axis=0).reshape(
            pairs_here, NCOUPLE, pair_width, pair_width
        )
        first_product = jnp.einsum(
            "psab,psbc->psac", intersection, partner_amplitudes, preferred_element_type=jnp.float32
        ).astype(jnp.bfloat16)
        second_product = jnp.einsum(
            "psac,psdc->psad", first_product, intersection, preferred_element_type=jnp.float32
        )
        coupled = jnp.einsum("psad,ps->pad", second_product, weights)
        residual = pair_integrals + local_terms - energy_shift[:, None, None] * current - coupled
        update = pair_mask * residual / denominators
        squares = lax.psum(jnp.sum(update * update), ("ia", "ja"))
        factor = jnp.minimum(1.0, clip_share * pair_width / jnp.sqrt(squares / total_pairs + 1e-06))
        current = current - factor * update
    return current.reshape(rows_here, columns_here, pair_width, pair_width)


def solution(mesh):
    return jax.shard_map(
        shards,
        mesh=mesh,
        in_specs=(
            P("ia", "ja", None, None),
            P("ia", "ja", None, None),
            P("ia", "ja", None, None),
            P(),
            P(),
            P("ja"),
            P(None, "ja"),
            P(None, "ja", None),
        ),
        out_specs=P("ia", "ja", None, None),
        check_vma=False,
    )
```

profile of v0, /device:TPU:12, one launch (start us, length us, event | category | flops | bytes accessed | tf_op | source)
XLA Modules:
  0.0 437.7 jit_solution(808519100536314652)
XLA Ops:
  0.0 0.8 copy.38
  0.8 0.8 constant_dynamic-slice_fusion.1
  1.6 0.1 copy.36
  1.7 0.1 reshape.383
  1.7 0.1 reshape.382
  1.9 0.3 convert_reduce_fusion
  2.2 0.2 select_reduce_fusion.1
  2.3 0.1 copy.39
  2.4 0.1 reshape.384
  2.5 0.8 dynamic-slice_multiply_fusion
  3.3 0.1 copy.33
  3.4 0.1 lt.91
  3.4 0.1 iota_compare_fusion.3
  3.5 1.4 fusion.29
  5.0 0.7 gather_fusion.4
  5.6 1.6 broadcast_select_fusion.4
  7.2 6.2 %all-to-all-start.1 = ((bf16[16,256,256]{2,1,0:T(8,128)(2,1)}), bf16[16,256,256]{2,1,0:T(8,128)(2,1)}, u32[]{:S(2)}, u32[]{:S(2)}) async-start(bf16[16,256,256]{2,1,0:T(8,128)(2,1)} %broadcast_select_fusion.4), calls=%async_computation.1 | async-start | bytes 4194304 | tf_op jit(solution)/shard_map/all_to_all | solution.py:89
  13.5 0.1 reshape.385
  13.6 0.1 compare_convert_fusion
  13.6 1.7 broadcast_multiply_fusion
  15.4 4.6 %gather_fusion.1 = bf16[16,1024,256]{2,1,0:T(8,128)(2,1)} fusion(bf16[4,1024,256]{2,1,0:T(8,128)(2,1)S(1)} %bitcast.57, s32[1024]{0:T(1024)S(1)} %pad_clamp_fusion.3), kind=kCustom, calls=%fused_computation.5 | custom fusion | bytes 16777280 | tf_op jit(solution)/shard_map/jit(_take)/gather | solution.py:78
  19.9 7.4 %broadcast_select_fusion = bf16[16,1024,256]{2,1,0:T(8,128)(2,1)} fusion(bf16[16,1024,256]{2,1,0:T(8,128)(2,1)} %gather_fusion.1, pred[16]{0:T(512)(128)(4,1)S(1)} %compare_and_fusion.1), kind=kLoop, calls=%fused_computation.10 | loop fusion | flops 4194304 | bytes 16777232 | tf_op jit(solution)/shard_map/jit(_take)/select_n | solution.py:78
  27.4 31.1 %all-to-all-done.1 = bf16[16,256,256]{2,1,0:T(8,128)(2,1)} async-done(((bf16[16,256,256]{2,1,0:T(8,128)(2,1)}), bf16[16,256,256]{2,1,0:T(8,128)(2,1)}, u32[]{:S(2)}, u32[]{:S(2)}) %all-to-all-start.1) | async-done | bytes 2097184 | tf_op jit(solution)/shard_map/all_to_all | solution.py:89
  58.4 8.2 %all-to-all-start = ((bf16[16,1024,256]{2,1,0:T(8,128)(2,1)}), bf16[16,1024,256]{2,1,0:T(8,128)(2,1)}, u32[]{:S(2)}, u32[]{:S(2)}) async-start(bf16[16,1024,256]{2,1,0:T(8,128)(2,1)} %broadcast_select_fusion), calls=%async_computation | async-start | bytes 16777216 | tf_op jit(solution)/shard_map/all_to_all | solution.py:79
  66.7 0.1 reshape.386
  66.7 2.2 fusion.42
  69.0 17.6 %copy.45 = f32[4,256,256]{0,2,1:T(8,128)} copy(f32[4,256,256]{2,1,0:T(8,128)} %get-tuple-element.14) | data formatting | bytes 2097152 | tf_op jit(solution)/shard_map/pxa,pxb->pab/dot_general | solution.py:69
  86.6 2.3 gather_fusion.3
  89.0 0.1 copy.46
  89.0 0.2 convert_reduce_fusion.1
  89.2 0.1 reduce_sum.59
  89.3 0.0 copy-done
  89.3 0.7 gather_fusion
  90.0 0.1 dynamic_slice.13
  90.1 0.1 broadcast_add_fusion
  90.1 0.1 add.186
  90.3 0.2 select_reduce_fusion
  90.5 1.3 fusion.43
  91.8 1.2 and_select_fusion.2
  93.0 3.6 gather_fusion.5
  96.6 3.2 broadcast_select_fusion.2
  99.8 145.9 %all-to-all-done = bf16[16,1024,256]{2,1,0:T(8,128)(2,1)} async-done(((bf16[16,1024,256]{2,1,0:T(8,128)(2,1)}), bf16[16,1024,256]{2,1,0:T(8,128)(2,1)}, u32[]{:S(2)}, u32[]{:S(2)}) %all-to-all-start) | async-done | bytes 8388640 | tf_op jit(solution)/shard_map/all_to_all | solution.py:79
  245.6 8.1 %gather_fusion.2 = bf16[16,1024,256]{2,1,0:T(8,128)(2,1)} fusion(bf16[16,1024,256]{2,1,0:T(8,128)(2,1)} %all-to-all-done, s32[1024]{0:T(1024)S(1)} %pad_clamp_fusion.2), kind=kCustom, calls=%fused_computation.6 | custom fusion | bytes 16777280 | tf_op jit(solution)/shard_map/jit(_take)/gather | solution.py:80
  253.8 12.3 %copy.42 = bf16[16,1024,256]{1,2,0:T(8,128)(2,1)} copy(bf16[16,1024,256]{2,1,0:T(8,128)(2,1)} %gather_fusion.2) | data formatting | bytes 16777216 | tf_op jit(solution)/shard_map/jit(_take)/gather | solution.py:80
  266.1 7.1 %fusion.18 = bf16[4,4,256,256]{3,2,1,0:T(8,128)(2,1)} fusion(bf16[4,1024,256,1]{2,1,3,0:T(8,128)(2,1)S(1)} %bitcast.59, bf16[4,4,1024,256]{2,3,1,0:T(8,128)(2,1)} %bitcast.61, pred[4,4]{1,0:T(4,128)(4,1)S(1)} %compare_and_fusion.2), kind=kOutput, calls=%fused_computation.30 | convolution fusion | flops 2152726528 | bytes 12582928 | tf_op jit(solution)/shard_map/pxa,psxb->psab/dot_general | solution.py:83
  273.2 4.2 fusion.13
  277.4 0.0 copy-start.6
  277.5 1.7 fusion.5
  279.2 0.1 copy-done.11
  279.3 1.8 multiply_reduce_fusion.1
  281.1 43.3 %psum.14 = f32[]{:T(128)} all-reduce(f32[]{:T(128)} %get-tuple-element.15), channel_id=1, replica_groups=mesh['ia'=8,'ja'=4] {'ia','ja'}, use_global_device_ids=true, to_apply=%region_5.8 | all-reduce | flops 1 | bytes 8 | tf_op jit(solution)/shard_map/psum | solution.py:110
  325.0 1.2 fusion.41
  326.2 0.7 gather_fusion.6
  326.9 1.6 broadcast_select_fusion.3
  328.5 4.3 all-to-all-start.2
  332.8 1.3 fusion.44
  334.1 42.8 %all-to-all-done.2 = bf16[16,256,256]{2,1,0:T(8,128)(2,1)S(1)} async-done(((bf16[16,256,256]{2,1,0:T(8,128)(2,1)}), bf16[16,256,256]{2,1,0:T(8,128)(2,1)S(1)}, u32[]{:S(2)}, u32[]{:S(2)}) %all-to-all-start.2) | async-done | bytes 2097184 | tf_op jit(solution)/shard_map/all_to_all | solution.py:89
  376.9 2.0 gather_fusion.7
  378.9 3.3 broadcast_select_fusion.1
  382.2 4.3 fusion.9
  386.5 3.4 fusion.3
  390.0 2.4 multiply_reduce_fusion
  392.4 42.2 %psum.15 = f32[]{:T(128)} all-reduce(f32[]{:T(128)} %get-tuple-element.17), channel_id=1, replica_groups=mesh['ia'=8,'ja'=4] {'ia','ja'}, use_global_device_ids=true, to_apply=%region_7.10 | all-reduce | flops 1 | bytes 8 | tf_op jit(solution)/shard_map/psum | solution.py:110
  435.3 2.5 multiply_subtract_fusion
  (40 shorter events, 0.2 us)
Async XLA Ops:
  0.0 89.3 %copy-start = (f32[16,16]{1,0:T(8,128)S(1)}, f32[16,16]{1,0:T(8,128)}, u32[]{:S(2)}) copy-start(f32[16,16]{1,0:T(8,128)} %param.16) | copy-start | bytes 3076
  7.2 51.2 %all-to-all-start.1 = ((bf16[16,256,256]{2,1,0:T(8,128)(2,1)}), bf16[16,256,256]{2,1,0:T(8,128)(2,1)}, u32[]{:S(2)}, u32[]{:S(2)}) async-start(bf16[16,256,256]{2,1,0:T(8,128)(2,1)} %broadcast_select_fusion.4), calls=%async_computation.1 | async-start | bytes 4194304 | tf_op jit(solution)/shard_map/all_to_all | solution.py:89
  27.4 39.4 %copy-start.9 = (f32[1024]{0:T(1024)S(1)}, f32[1024]{0:T(1024)}, u32[]{:S(2)}) copy-start(f32[1024]{0:T(1024)} %param.15) | copy-start | bytes 12292
  58.4 187.2 %all-to-all-start = ((bf16[16,1024,256]{2,1,0:T(8,128)(2,1)}), bf16[16,1024,256]{2,1,0:T(8,128)(2,1)}, u32[]{:S(2)}, u32[]{:S(2)}) async-start(bf16[16,1024,256]{2,1,0:T(8,128)(2,1)} %broadcast_select_fusion), calls=%async_computation | async-start | bytes 16777216 | tf_op jit(solution)/shard_map/all_to_all | solution.py:79
  69.0 21.1 %copy-start.10 = (f32[2]{0:T(128)S(1)}, f32[2]{0:T(128)}, u32[]{:S(2)}) copy-start(f32[2]{0:T(128)} %param.17) | copy-start | bytes 28
  90.2 1.6 copy-start.3
  277.4 1.7 copy-start.6
  277.4 1.7 copy-start.7
  277.4 1.8 copy-start.11
  279.3 45.7 %copy-start.4 = (f32[2,2,256,256]{3,2,1,0:T(8,128)S(1)}, f32[2,2,256,256]{3,2,1,0:T(8,128)}, u32[]{:S(2)}) copy-start(f32[2,2,256,256]{3,2,1,0:T(8,128)} %param.13) | copy-start | bytes 3145732
  328.5 48.4 %all-to-all-start.2 = ((bf16[16,256,256]{2,1,0:T(8,128)(2,1)}), bf16[16,256,256]{2,1,0:T(8,128)(2,1)S(1)}, u32[]{:S(2)}, u32[]{:S(2)}) async-start(bf16[16,256,256]{2,1,0:T(8,128)(2,1)} %broadcast_select_fusion.3), calls=%async_computation.2 | async-start | bytes 4194304 | tf_op jit(solution)/shard_map/all_to_all | solution.py:89
  378.9 3.3 copy-start.2
  386.5 3.5 copy-start.5
  386.5 3.5 copy-start.8
  386.5 3.5 copy-start.12
  390.0 47.7 %copy-start.1 = (f32[16,16]{1,0:T(8,128)S(1)}, f32[16,16]{1,0:T(8,128)}, u32[]{:S(2)}) copy-start(f32[16,16]{1,0:T(8,128)} %param.16) | copy-start | bytes 3076
where the time goes:
time: 439 us; the launch traced here: 438 us
  waiting for transfers between devices  220 us (50%)
  blocking collectives  85.4 us (19%)
  local copies, waits for them, and re-layouts  55.4 us (13%)
  matrix products  29.8 us (7%)
  other arithmetic  27 us (6%)
  starting transfers between devices  18.7 us (4%)
    all_to_all x1, waiting for transfers between devices, shards(): lax.all_to_all(sent_bases, 'ia', split_axis=0, concat_axis=0, tiled=True)  146 us
    psum x2, blocking collectives, shards(): squares = lax.psum(jnp.sum(update * update), ('ia', 'ja'))  85.4 us
    all_to_all x2, waiting for transfers between devices, shards(): lax.all_to_all(sent_amplitudes, 'ia', split_axis=0, concat_axis=0, tiled=...  73.9 us
    gather x2, local copies, waits for them, and re-layouts, shards(): jnp.take(arrived_bases, arrival, axis=0)  20.5 us
    dot_general x1, local copies, waits for them, and re-layouts, shards(): jnp.einsum('pxa,pxb->pab', masked, scaled, preferred_element_type=jnp.flo...  17.6 us
    all_to_all x2, starting transfers between devices, shards(): lax.all_to_all(sent_amplitudes, 'ia', split_axis=0, concat_axis=0, tiled=...  10.5 us
  transfers between devices with their start and end apart: 3, of which 3 were waited for; matrix products, arithmetic and copies ran while one was open for 11% of the time, Pallas kernels for 0%

commit v1 on v0

v1 whole, which is shorter than its diff:
```python
import functools

import jax
import jax.numpy as jnp
from jax import lax
from jax.experimental import pallas as pl
from jax.experimental.pallas import tpu as pltpu
from jax.sharding import PartitionSpec as P

BLOCK = 128
NCOUPLE = 4
SWEEPS = 2
MESH = pl.DeviceIdType.MESH

clip_share = 0.4
denominator_floor = 1.0


def rank_within(block_ids):
    entries = block_ids.shape[-1]
    matching = block_ids[..., :, None] == block_ids[..., None, :]
    earlier = jnp.arange(entries)[:, None] > jnp.arange(entries)[None, :]
    return jnp.sum((matching & earlier).astype(jnp.int32), axis=-1)


def total_kernel(n_ia, n_ja, x_ref, o_ref, near, far, near_send, near_recv, far_send, far_recv, own_sem):
    ia, ja = lax.axis_index("ia"), lax.axis_index("ja")
    barrier = pltpu.get_barrier_semaphore()
    for step in range(1, n_ja):
        pl.semaphore_signal(barrier, inc=1, device_id=(ia, lax.rem(ja + step, n_ja)), device_id_type=MESH)
    for step in range(1, n_ia):
        pl.semaphore_signal(barrier, inc=1, device_id=(lax.rem(ia + step, n_ia), ja), device_id_type=MESH)
    own = pltpu.make_async_copy(x_ref, near.at[0], own_sem)
    own.start()
    pl.semaphore_wait(barrier, n_ja + n_ia - 2)
    copies = []
    for step in range(1, n_ja):
        copy = pltpu.make_async_remote_copy(
            src_ref=x_ref,
            dst_ref=near.at[step],
            send_sem=near_send.at[step],
            recv_sem=near_recv.at[step],
            device_id=(ia, lax.rem(ja + step, n_ja)),
            device_id_type=MESH,
        )
        copy.start()
        copies.append(copy)
    own.wait()
    for copy in copies:
        copy.wait()
    copies = []
    for step in range(1, n_ia):
        copy = pltpu.make_async_remote_copy(
            src_ref=near,
            dst_ref=far.at[step - 1],
            send_sem=far_send.at[step],
            recv_sem=far_recv.at[step],
            device_id=(lax.rem(ia + step, n_ia), ja),
            device_id_type=MESH,
        )
        copy.start()
        copies.append(copy)
    for copy in copies:
        copy.wait()
    o_ref[...] = jnp.sum(near[...], axis=0) + jnp.sum(far[...].reshape(((n_ia - 1) * n_ja,) + o_ref.shape), axis=0)


def total_of(x, n_ia, n_ja, call):
    shape = x.shape
    return pl.pallas_call(
        functools.partial(total_kernel, n_ia, n_ja),
        out_shape=jax.ShapeDtypeStruct(shape, jnp.float32),
        in_specs=[pl.BlockSpec(memory_space=pltpu.VMEM)],
        out_specs=pl.BlockSpec(memory_space=pltpu.VMEM),
        scratch_shapes=[
            pltpu.VMEM((n_ja,) + shape, jnp.float32),
            pltpu.VMEM((n_ia - 1, n_ja) + shape, jnp.float32),
            pltpu.SemaphoreType.DMA((n_ja,)),
            pltpu.SemaphoreType.DMA((n_ja,)),
            pltpu.SemaphoreType.DMA((n_ia,)),
            pltpu.SemaphoreType.DMA((n_ia,)),
            pltpu.SemaphoreType.DMA,
        ],
        compiler_params=pltpu.CompilerParams(collective_id=call, has_side_effects=True),
        name="total" + str(call),
    )(x)


def live_rows(shape, live):
    return lax.broadcasted_iota(jnp.int32, shape, 0) < live


def live_columns(shape, live):
    return lax.broadcasted_iota(jnp.int32, shape, 1) < live


def virtual_kernel(live, shift, basis, energy, virtual, denominators):
    p = pl.program_id(0)
    width = basis.shape[2]
    own = basis[0]
    scaled = (own.astype(jnp.float32) * energy[...]).astype(jnp.bfloat16)
    full = jnp.dot(own.T, scaled, preferred_element_type=jnp.float32)
    both = live_rows(full.shape, live[p]) & live_columns(full.shape, live[p])
    full = jnp.where(both, full, 0.0)
    virtual[0] = full.astype(jnp.bfloat16)
    same = lax.broadcasted_iota(jnp.int32, full.shape, 0) == lax.broadcasted_iota(jnp.int32, full.shape, 1)
    picked = jnp.where(same, full, 0.0)
    down = jnp.sum(picked, axis=1, keepdims=True)
    across = jnp.sum(picked, axis=0, keepdims=True)
    denominators[0] = jnp.maximum(down + across - shift[p], denominator_floor)


def virtual_of(basis, energy, live, shift):
    pairs, projected, width = basis.shape
    return pl.pallas_call(
        virtual_kernel,
        out_shape=(
            jax.ShapeDtypeStruct((pairs, width, width), jnp.bfloat16),
            jax.ShapeDtypeStruct((pairs, width, width), jnp.float32),
        ),
        grid_spec=pltpu.PrefetchScalarGridSpec(
            num_scalar_prefetch=2,
            grid=(pairs,),
            in_specs=[
                pl.BlockSpec((1, projected, width), lambda p, *_: (p, 0, 0)),
                pl.BlockSpec((projected, 1), lambda p, *_: (0, 0)),
            ],
            out_specs=[pl.BlockSpec((1, width, width), lambda p, *_: (p, 0, 0))] * 2,
        ),
        cost_estimate=pl.CostEstimate(flops=2 * pairs * projected * width * width, bytes_accessed=4 * pairs * projected * width, transcendentals=0),
    )(live, shift, basis, energy)


def overlap_kernel(arrival, live, live_partner, own, partner, out, turned):
    p, s = pl.program_id(0), pl.program_id(1)

    @pl.when(s == 0)
    def _():
        turned[...] = own[0].T

    full = jnp.dot(turned[...], partner[0], preferred_element_type=jnp.float32)
    both = live_rows(full.shape, live[p]) & live_columns(full.shape, live_partner[p * NCOUPLE + s])
    out[0] = jnp.where(both, full, 0.0).astype(jnp.bfloat16)


def overlap_of(basis, arrived, arrival, live, live_partner):
    pairs, projected, width = basis.shape
    return pl.pallas_call(
        overlap_kernel,
        out_shape=jax.ShapeDtypeStruct((pairs * NCOUPLE, width, width), jnp.bfloat16),
        grid_spec=pltpu.PrefetchScalarGridSpec(
            num_scalar_prefetch=3,
            grid=(pairs, NCOUPLE),
            in_specs=[
                pl.BlockSpec((1, projected, width), lambda p, s, *_: (p, 0, 0)),
                pl.BlockSpec((1, projected, width), lambda p, s, a, *_: (a[p * NCOUPLE + s], 0, 0)),
            ],
            out_specs=pl.BlockSpec((1, width, width), lambda p, s, *_: (p * NCOUPLE + s, 0, 0)),
            scratch_shapes=[pltpu.VMEM((width, projected), jnp.bfloat16)],
        ),
    )(arrival, live, live_partner, basis, arrived)


def sweep_kernel(arrival, live, weights, shift, overlap, partner, virtual, denominators, current, integrals, update, squares, coupled):
    p, s = pl.program_id(0), pl.program_id(1)
    first = jnp.dot(overlap[0], partner[0], preferred_element_type=jnp.float32).astype(jnp.bfloat16)
    second = lax.dot_general(first, overlap[0], (((1,), (1,)), ((), ())), preferred_element_type=jnp.float32)
    term = weights[p * NCOUPLE + s] * second

    @pl.when(s == 0)
    def _():
        coupled[...] = term

    @pl.when(s > 0)
    def _():
        coupled[...] += term

    @pl.when(s == NCOUPLE - 1)
    def _():
        rounded = current[0].astype(jnp.bfloat16)
        residual = integrals[0] + jnp.dot(virtual[0], rounded, preferred_element_type=jnp.float32)
        residual = residual + jnp.dot(rounded, virtual[0], preferred_element_type=jnp.float32)
        residual = residual - shift[p] * current[0] - coupled[...]
        both = live_rows(residual.shape, live[p]) & live_columns(residual.shape, live[p])
        change = jnp.where(both, residual, 0.0) / denominators[0]
        update[0] = change
        squared = change * change
        height, width = squared.shape
        part = jnp.sum(squared.reshape(height // 8, 8, width), axis=0)
        folded = part[:, :128]
        for start in range(128, width, 128):
            folded = folded + part[:, start : start + 128]

        @pl.when(p == 0)
        def _():
            squares[...] = folded

        @pl.when(p > 0)
        def _():
            squares[...] += folded


def sweep_of(overlap, arrived, arrival, live, weights, shift, virtual, denominators, current, integrals):
    pairs, width, _ = current.shape
    wide = pl.BlockSpec((1, width, width), lambda p, s, *_: (p, 0, 0))
    return pl.pallas_call(
        sweep_kernel,
        out_shape=(
            jax.ShapeDtypeStruct((pairs, width, width), jnp.float32),
            jax.ShapeDtypeStruct((8, 128), jnp.float32),
        ),
        grid_spec=pltpu.PrefetchScalarGridSpec(
            num_scalar_prefetch=4,
            grid=(pairs, NCOUPLE),
            in_specs=[
                pl.BlockSpec((1, width, width), lambda p, s, *_: (p * NCOUPLE + s, 0, 0)),
                pl.BlockSpec((1, width, width), lambda p, s, a, *_: (a[p * NCOUPLE + s], 0, 0)),
                wide,
                wide,
                wide,
                wide,
            ],
            out_specs=[wide, pl.BlockSpec((8, 128), lambda p, s, *_: (0, 0))],
            scratch_shapes=[pltpu.VMEM((width, width), jnp.float32)],
        ),
    )(arrival, live, weights, shift, overlap, arrived, virtual, denominators, current, integrals)


def gather_kernel(sources, x, out):
    out[...] = x[...]


def gather_of(x, sources):
    count = sources.shape[0]
    rows, width = x.shape[1:]
    return pl.pallas_call(
        gather_kernel,
        out_shape=jax.ShapeDtypeStruct((count, rows, width), x.dtype),
        grid_spec=pltpu.PrefetchScalarGridSpec(
            num_scalar_prefetch=1,
            grid=(count,),
            in_specs=[pl.BlockSpec((1, rows, width), lambda n, a: (a[n], 0, 0))],
            out_specs=pl.BlockSpec((1, rows, width), lambda n, a: (n, 0, 0)),
        ),
    )(sources, x)


def shards(basis, amplitudes, integrals, virt_energy, fock, occ_energy, blocks, couplings):
    rows_here, columns_here, projected, pair_width = basis.shape
    pairs_here = rows_here * columns_here
    requests = NCOUPLE * pairs_here
    row_groups = lax.axis_size("ia")
    column_groups = lax.axis_size("ja")
    slot_count = requests // row_groups
    group_index = lax.axis_index("ia")
    first_row = group_index * rows_here
    total_pairs = rows_here * row_groups * columns_here * column_groups
    live = lax.dynamic_slice_in_dim(blocks, first_row, rows_here, 0).reshape(pairs_here) * BLOCK
    orbital_index = jnp.arange(pair_width, dtype=jnp.int32)
    column_mask = orbital_index[None, :] < live[:, None]
    pair_mask = column_mask[:, :, None] & column_mask[:, None, :]
    local_couplings = lax.dynamic_slice_in_dim(couplings, first_row, rows_here, 0)
    local_targets = local_couplings.reshape(requests) // rows_here
    arrival = local_targets * slot_count + rank_within(local_targets)
    all_couplings = couplings.reshape(row_groups, requests)
    all_targets = all_couplings // rows_here
    all_ranks = rank_within(all_targets)
    pair_column = jnp.arange(requests, dtype=jnp.int32) // NCOUPLE % columns_here
    source_pair = (all_couplings - first_row) * columns_here + pair_column[None, :]
    slot_index = jnp.arange(slot_count, dtype=jnp.int32)
    chosen = (all_targets == group_index)[:, :, None] & (
        all_ranks[:, :, None] == slot_index[None, None, :]
    )
    sources = jnp.sum(chosen.astype(jnp.int32) * source_pair[:, :, None], axis=1).reshape(
        row_groups * slot_count
    )
    fock_rows = lax.dynamic_slice_in_dim(fock, first_row, rows_here, 0)
    picked = local_couplings[:, :, :, None] == jnp.arange(fock.shape[1], dtype=jnp.int32)
    weights = jnp.sum(jnp.where(picked, fock_rows[:, None, None, :], 0.0), axis=-1).reshape(requests)
    live_partner = BLOCK * jnp.sum(
        jnp.where(picked, blocks.T[None, :, None, :], 0), axis=-1
    ).reshape(requests)
    occupied_diag = lax.dynamic_slice_in_dim(jnp.diagonal(fock), first_row, rows_here, 0)
    shift = (occupied_diag[:, None] + occ_energy[None, :]).reshape(pairs_here)
    bases = basis.reshape(pairs_here, projected, pair_width)
    current = jnp.where(pair_mask, amplitudes.reshape(pairs_here, pair_width, pair_width), 0.0)
    pair_integrals = integrals.reshape(pairs_here, pair_width, pair_width)
    arrived_bases = lax.all_to_all(
        gather_of(bases, sources), "ia", split_axis=0, concat_axis=0, tiled=True
    )
    virtual, denominators = virtual_of(bases, virt_energy[:, None], live, shift)
    overlap = overlap_of(bases, arrived_bases, arrival, live, live_partner)
    for sweep_index in range(SWEEPS):
        arrived = lax.all_to_all(
            gather_of(current.astype(jnp.bfloat16), sources), "ia", split_axis=0, concat_axis=0, tiled=True
        )
        update, squares = sweep_of(
            overlap, arrived, arrival, live, weights, shift, virtual, denominators, current, pair_integrals
        )
        squares = jnp.sum(total_of(squares, row_groups, column_groups, sweep_index))
        factor = jnp.minimum(1.0, clip_share * pair_width / jnp.sqrt(squares / total_pairs + 1e-06))
        current = current - factor * update
    return current.reshape(rows_here, columns_here, pair_width, pair_width)


def solution(mesh):
    return jax.shard_map(
        shards,
        mesh=mesh,
        in_specs=(
            P("ia", "ja", None, None),
            P("ia", "ja", None, None),
            P("ia", "ja", None, None),
            P(),
            P(),
            P("ja"),
            P(None, "ja"),
            P(None, "ja", None),
        ),
        out_specs=P("ia", "ja", None, None),
        check_vma=False,
    )
```

time: 439 us -> 384 us (0.87)
  Pallas kernels: 0 us -> 109 us
  local copies, waits for them, and re-layouts: 55.4 us -> 7.05 us
  blocking collectives: 85.4 us -> 51 us
  waiting for transfers between devices: 220 us -> 188 us
  matrix products: 29.8 us -> 0 us
  other arithmetic: 27 us -> 10.8 us
  starting transfers between devices: 18.7 us -> 13.5 us
    pallas_call x0 -> x9, Pallas kernels: none -> 109 us  [the longest x3 32.9 us: gather_of(): pl.pallas_call(gather_kernel, out_shape=jax.ShapeDtypeStruct((count, rows...]
    psum x2 -> x0, blocking collectives: 85.4 us -> none  [shards(): squares = lax.psum(jnp.sum(update * update), ('ia', 'ja'))]
    all_to_all x0 -> x1, blocking collectives: none -> 51 us  [shards(): lax.all_to_all(gather_of(current.astype(jnp.bfloat16), sources), 'ia', sp...]
    gather x9 -> x0, local copies, waits for them, and re-layouts: 34.4 us -> none  [the longest x2 20.5 us: shards(): jnp.take(arrived_bases, arrival, axis=0)]
    all_to_all x3 -> x2, waiting for transfers between devices: 220 us -> 188 us  [the longest x1 168 us: shards(): lax.all_to_all(gather_of(bases, sources), 'ia', split_axis=0, concat_axis...]
    dot_general x10 -> x0, matrix products: 29.8 us -> none  [the longest x2 8.51 us: shards(): jnp.einsum('psac,psdc->psad', first_product, intersection, preferred_elem...]
    dot_general x1 -> x0, local copies, waits for them, and re-layouts: 17.6 us -> none  [shards(): jnp.einsum('pxa,pxb->pab', masked, scaled, preferred_element_type=jnp.flo...]
    select_n x8 -> x1, other arithmetic: 17.1 us -> 0.01 us  [shards(): local_targets = local_couplings.reshape(requests) // rows_here]
  transfers between devices with their start and end apart: 3 -> 2, of which waited for: 3 -> 2; matrix products, arithmetic and copies ran while one was open for 11% -> 2% of each run, Pallas kernels for 0% -> 8%
where the time goes in v1:
time: 384 us; the launch traced here: 380 us
  waiting for transfers between devices  188 us (49%)
  Pallas kernels  109 us (28%)
  blocking collectives  51 us (13%)
  starting transfers between devices  13.5 us (4%)
  other arithmetic  10.8 us (3%)
  local copies, waits for them, and re-layouts  7.05 us (2%)
    all_to_all x1, waiting for transfers between devices, shards(): lax.all_to_all(gather_of(bases, sources), 'ia', split_axis=0, concat_axis...  168 us
    all_to_all x1, blocking collectives, shards(): lax.all_to_all(gather_of(current.astype(jnp.bfloat16), sources), 'ia', sp...  51 us
    pallas_call x3, Pallas kernels, gather_of(): pl.pallas_call(gather_kernel, out_shape=jax.ShapeDtypeStruct((count, rows...  32.9 us
    pallas_call x2, Pallas kernels, sweep_of(): pl.pallas_call(sweep_kernel, out_shape=(jax.ShapeDtypeStruct((pairs, widt...  29.6 us
    pallas_call x2, Pallas kernels, total_of(): pl.pallas_call(functools.partial(total_kernel, n_ia, n_ja), out_shape=jax...  26 us
    all_to_all x1, waiting for transfers between devices, shards(): lax.all_to_all(gather_of(current.astype(jnp.bfloat16), sources), 'ia', sp...  19.8 us
    pallas_call x1, Pallas kernels, overlap_of(): pl.pallas_call(overlap_kernel, out_shape=jax.ShapeDtypeStruct((pairs * NC...  14.7 us
  transfers between devices with their start and end apart: 2, of which 2 were waited for; matrix products, arithmetic and copies ran while one was open for 2% of the time, Pallas kernels for 8%

profile of v1, /device:TPU:12, one launch (start us, length us, event | category | flops | bytes accessed | tf_op | source)
XLA Modules:
  0.0 380.2 jit_solution(16730852328565619125)
XLA Ops:
  0.0 0.0 copy-start
  0.0 0.8 copy.21
  0.8 0.1 reshape.263
  0.9 0.3 convert_reduce_fusion
  1.2 0.2 select_reduce_fusion
  1.4 0.1 copy.22
  1.4 0.6 reshape.264.sources
  2.1 12.7 %shard_map.82 = bf16[16,1024,256]{2,1,0:T(8,128)(2,1)} custom-call(s32[16]{0:T(128)} %reshape.264.sources, bf16[4,1024,256]{2,1,0:T(8,128)(2,1)} %bitcast.10), custom_call_target="tpu_custom_call" | custom-call | tf_op jit(solution)/shard_map/pallas_call | solution.py:236
  14.8 0.0 copy-start.8
  14.8 0.0 copy-start.4
  14.8 6.5 %all-to-all-start = ((bf16[16,1024,256]{2,1,0:T(8,128)(2,1)}), bf16[16,1024,256]{2,1,0:T(8,128)(2,1)}, u32[]{:S(2)}, u32[]{:S(2)}) async-start(bf16[16,1024,256]{2,1,0:T(8,128)(2,1)} %shard_map.82), calls=%async_computation | async-start | bytes 16777216 | tf_op jit(solution)/shard_map/all_to_all | solution.py:288
  21.3 0.0 copy-done.8
  21.3 0.1 dynamic-slice_multiply_fusion
  21.4 0.1 copy.18
  21.5 0.1 mul.46.live
  21.6 0.0 copy-start.6
  21.6 0.1 iota_compare_fusion.3
  21.6 0.0 copy-done.4
  21.6 1.4 fusion.5
  23.0 10.1 %shard_map.84 = bf16[16,256,256]{2,1,0:T(8,128)(2,1)} custom-call(s32[16]{0:T(128)} %reshape.264.sources, bf16[4,256,256]{2,1,0:T(8,128)(2,1)} %get-tuple-element.19.x), custom_call_target="tpu_custom_call" | custom-call | tf_op jit(solution)/shard_map/pallas_call | solution.py:236
  33.1 0.0 copy-done.6
  33.1 0.0 copy-start.5
  33.1 0.0 copy-start.9
  33.1 0.0 copy-start.7
  33.2 167.9 %all-to-all-done.partner = bf16[16,1024,256]{2,1,0:T(8,128)(2,1)} async-done(((bf16[16,1024,256]{2,1,0:T(8,128)(2,1)}), bf16[16,1024,256]{2,1,0:T(8,128)(2,1)}, u32[]{:S(2)}, u32[]{:S(2)}) %all-to-all-start) | async-done | bytes 8388640 | tf_op jit(solution)/shard_map/all_to_all | solution.py:288
  201.1 7.0 %all-to-all-start.1 = ((bf16[16,256,256]{2,1,0:T(8,128)(2,1)}), bf16[16,256,256]{2,1,0:T(8,128)(2,1)S(1)}, u32[]{:S(2)}, u32[]{:S(2)}) async-start(bf16[16,256,256]{2,1,0:T(8,128)(2,1)} %shard_map.84), calls=%async_computation.1 | async-start | bytes 4194304 | tf_op jit(solution)/shard_map/all_to_all | solution.py:294
  208.1 0.0 copy-done.5
  208.1 0.1 constant_dynamic-slice_fusion.1
  208.2 0.1 copy.19
  208.3 0.1 reshape.260
  208.4 0.2 select_reduce_fusion.1
  208.6 0.6 mul.49.live_partner
  209.2 0.0 copy-done
  209.2 0.7 gather_fusion
  209.9 0.1 dynamic_slice.15
  209.9 0.0 copy-done.9
  209.9 0.1 broadcast_add_fusion
  210.0 0.6 add.89.shift
  210.6 0.0 copy-done.7
  210.7 1.1 copy.23.energy
  211.7 0.2 select_reduce_fusion.2
  211.9 0.6 reshape.261.weights
  212.5 5.5 %shard_map.85 = (bf16[4,256,256]{2,1,0:T(8,128)(2,1)}, f32[4,256,256]{2,1,0:T(8,128)}) custom-call(s32[4]{0:T(128)} %copy-done.6, f32[4]{0:T(128)} %add.89.shift, bf16[4,1024,256]{2,1,0:T(8,128)(2,1)} %bitcast.11, f32[1024,1]{1,0:T(8,128)} %copy.23.energy), custom_call_target="tpu_custom_call" | custom-call | flops 536870912 | bytes 4194304 | tf_op jit(solution)/shard_map/pallas_call | solution.py:115
  218.0 0.2 convert_reduce_fusion.1
  218.2 0.5 multiply_add_fusion.1.arrival
  218.7 14.7 %shard_map.83.overlap = bf16[16,256,256]{2,1,0:T(8,128)(2,1)} custom-call(s32[16]{0:T(128)} %multiply_add_fusion.1.arrival, s32[4]{0:T(128)} %copy-done.6, s32[16]{0:T(128)} %mul.49.live_partner, bf16[4,1024,256]{2,1,0:T(8,128)(2,1)} %bitcast.12, bf16[16,1024,256]{2,1,0:T(8,128)(2,1)} %all-to-all-done.partner), custom_call_target="tpu_custom_call" | custom-call | tf_op jit(solution)/shard_map/pallas_call | solution.py:148
  233.5 19.8 %all-to-all-done.1.partner = bf16[16,256,256]{2,1,0:T(8,128)(2,1)S(1)} async-done(((bf16[16,256,256]{2,1,0:T(8,128)(2,1)}), bf16[16,256,256]{2,1,0:T(8,128)(2,1)S(1)}, u32[]{:S(2)}, u32[]{:S(2)}) %all-to-all-start.1) | async-done | bytes 2097184 | tf_op jit(solution)/shard_map/all_to_all | solution.py:294
  253.2 0.0 copy-start.3
  253.2 1.3 copy-done.3
  254.6 0.0 copy-start.1
  254.6 14.8 %shard_map.86 = (f32[4,256,256]{2,1,0:T(8,128)}, f32[8,128]{1,0:T(8,128)}) custom-call(s32[16]{0:T(128)} %multiply_add_fusion.1.arrival, s32[4]{0:T(128)} %copy-done.6, f32[16]{0:T(128)} %reshape.261.weights, f32[4]{0:T(128)} %add.89.shift, bf16[16,256,256]{2,1,0:T(8,128)(2,1)} %shard_map.83.overlap, bf16[16,256,256]{2,1,0:T(8,128)(2,1)} %copy-done.3, ...), custom_call_target="tpu_custom_call" | custom-call | tf_op jit(solution)/shard_map/pallas_call | solution.py:206
  269.4 13.9 %total0.1 = f32[8,128]{1,0:T(8,128)} custom-call(f32[8,128]{1,0:T(8,128)} %get-tuple-element.13.x_ref), custom_call_target="tpu_custom_call" | custom-call | tf_op jit(solution)/shard_map/total0/pallas_call | solution.py:70
  283.3 1.3 reduce_sum.68
  285.3 0.0 copy-done.1
  285.3 2.6 fusion.4
  287.9 10.1 %shard_map.87 = bf16[16,256,256]{2,1,0:T(8,128)(2,1)} custom-call(s32[16]{0:T(128)} %reshape.264.sources, bf16[4,256,256]{2,1,0:T(8,128)(2,1)} %get-tuple-element.17.x), custom_call_target="tpu_custom_call" | custom-call | tf_op jit(solution)/shard_map/pallas_call | solution.py:236
  298.0 51.0 %all_to_all.15.partner = bf16[16,256,256]{2,1,0:T(8,128)(2,1)} all-to-all(bf16[16,256,256]{2,1,0:T(8,128)(2,1)} %shard_map.87), channel_id=1, replica_groups=mesh['ia'=8,'ja'=4] {'ia'}, dimensions={0} | all-to-all | bytes 4194304 | tf_op jit(solution)/shard_map/all_to_all | solution.py:294
  349.0 0.0 copy-start.2
  349.0 14.8 %shard_map.88 = (f32[4,256,256]{2,1,0:T(8,128)}, f32[8,128]{1,0:T(8,128)}) custom-call(s32[16]{0:T(128)} %multiply_add_fusion.1.arrival, s32[4]{0:T(128)} %copy-done.6, f32[16]{0:T(128)} %reshape.261.weights, f32[4]{0:T(128)} %add.89.shift, bf16[16,256,256]{2,1,0:T(8,128)(2,1)} %shard_map.83.overlap, bf16[16,256,256]{2,1,0:T(8,128)(2,1)} %all_to_all.15.partner, ...), custom_call_target="tpu_custom_call" | custom-call | tf_op jit(solution)/shard_map/pallas_call | solution.py:206
  363.8 12.0 %total1.1 = f32[8,128]{1,0:T(8,128)} custom-call(f32[8,128]{1,0:T(8,128)} %get-tuple-element.15.x_ref), custom_call_target="tpu_custom_call" | custom-call | tf_op jit(solution)/shard_map/total1/pallas_call | solution.py:70
  375.8 1.3 reduce_sum.69
  377.7 0.0 copy-done.2
  377.7 2.5 multiply_subtract_fusion
  (8 shorter events, 0.1 us)
Async XLA Ops:
  0.0 209.2 %copy-start = (f32[16,16]{1,0:T(8,128)S(1)}, f32[16,16]{1,0:T(8,128)}, u32[]{:S(2)}) copy-start(f32[16,16]{1,0:T(8,128)} %param.12) | copy-start | bytes 3076
  14.8 6.5 %copy-start.8 = (s32[16,2]{0,1:T(2,128)S(1)}, s32[16,2]{0,1:T(2,128)}, u32[]{:S(2)}) copy-start(s32[16,2]{0,1:T(2,128)} %param.14) | copy-start | bytes 388
  14.8 6.9 %copy-start.4 = (f32[2,2,256,256]{3,2,1,0:T(8,128)S(1)}, f32[2,2,256,256]{3,2,1,0:T(8,128)}, u32[]{:S(2)}) copy-start(f32[2,2,256,256]{3,2,1,0:T(8,128)} %param.9) | copy-start | bytes 3145732
  14.8 186.3 %all-to-all-start = ((bf16[16,1024,256]{2,1,0:T(8,128)(2,1)}), bf16[16,1024,256]{2,1,0:T(8,128)(2,1)}, u32[]{:S(2)}, u32[]{:S(2)}) async-start(bf16[16,1024,256]{2,1,0:T(8,128)(2,1)} %shard_map.82), calls=%async_computation | async-start | bytes 16777216 | tf_op jit(solution)/shard_map/all_to_all | solution.py:288
  21.6 11.6 %copy-start.6 = (s32[4]{0:T(128)}, s32[4]{0:T(128)S(1)}, u32[]{:S(2)}) copy-start(s32[4]{0:T(128)S(1)} %mul.46.live) | copy-start | bytes 52
  33.1 175.0 %copy-start.5 = (s32[16,2,4]{0,2,1:T(4,128)S(1)}, s32[16,2,4]{0,2,1:T(4,128)}, u32[]{:S(2)}) copy-start(s32[16,2,4]{0,2,1:T(4,128)} %param.15) | copy-start | bytes 1540
  33.1 176.8 %copy-start.9 = (f32[2]{0:T(128)S(1)}, f32[2]{0:T(128)}, u32[]{:S(2)}) copy-start(f32[2]{0:T(128)} %param.13) | copy-start | bytes 28
  33.1 177.5 %copy-start.7 = (f32[1024]{0:T(1024)S(1)}, f32[1024]{0:T(1024)}, u32[]{:S(2)}) copy-start(f32[1024]{0:T(1024)} %param.11) | copy-start | bytes 12292
  201.1 52.2 %all-to-all-start.1 = ((bf16[16,256,256]{2,1,0:T(8,128)(2,1)}), bf16[16,256,256]{2,1,0:T(8,128)(2,1)S(1)}, u32[]{:S(2)}, u32[]{:S(2)}) async-start(bf16[16,256,256]{2,1,0:T(8,128)(2,1)} %shard_map.84), calls=%async_computation.1 | async-start | bytes 4194304 | tf_op jit(solution)/shard_map/all_to_all | solution.py:294
  253.2 1.4 copy-start.3
  254.6 30.7 %copy-start.1 = (f32[4,256,256]{2,1,0:T(8,128)S(1)}, f32[4,256,256]{2,1,0:T(8,128)}, u32[]{:S(2)}) copy-start(f32[4,256,256]{2,1,0:T(8,128)} %get-tuple-element.20.current) | copy-start | bytes 3145732
  349.0 28.7 %copy-start.2 = (f32[4,256,256]{2,1,0:T(8,128)S(1)}, f32[4,256,256]{2,1,0:T(8,128)}, u32[]{:S(2)}) copy-start(f32[4,256,256]{2,1,0:T(8,128)} %get-tuple-element.18.current) | copy-start | bytes 3145732
